TPU v7x, 32 devices: a whole 2x2x4 slice. The times are simulated.
32 devices in a mesh: seq: 8 (over y, x, core), tp: 4 (over z).
Axes of the slice: x: 2, y: 2, z: 4, core: 2. Of those that a mesh axis runs over, the one named last changes fastest.
Arguments:
- tokens: bfloat16 [128, 17, 1152], P('seq'), may hold values from -6 to 6
- cotangent: bfloat16 [128, 17, 1152], P('seq'), may hold values from -6 to 6
- caption: bfloat16 [4, 300, 1152], replicated, may hold values from -6 to 6
- condition: float32 [4, 1152], replicated, may hold values from -6 to 6
- frames: int32 [4], replicated, may hold values from 1 to 17, 44 in all
- cap_len: int32 [4], replicated, may hold values from 1 to 300, 600 in all
- clip_of: int32 [128], P('seq'), may hold values from 0 to 3
- w_qkv: bfloat16 [1152, 3, 1152], P('seq', None, 'tp'), may hold values from -0.1875 to 0.1875
- w_out: bfloat16 [1152, 1152], P('tp', 'seq'), may hold values from -0.375 to 0.375
- w_query2: bfloat16 [1152, 1152], P('seq', 'tp'), may hold values from -0.1875 to 0.1875
- w_kv2: bfloat16 [1152, 2, 1152], P('seq', None, 'tp'), may hold values from -0.1875 to 0.1875
- w_out2: bfloat16 [1152, 1152], P('tp', 'seq'), may hold values from -0.75 to 0.75
- w_up: bfloat16 [1152, 4608], P('seq', 'tp'), may hold values from -0.1875 to 0.1875
- w_down: bfloat16 [4608, 1152], P('tp', 'seq'), may hold values from -0.09375 to 0.09375
- w_ada: bfloat16 [1152, 6912], P('seq', 'tp'), may hold values from -0.1875 to 0.1875
Outputs:
- output: bfloat16 [128, 17, 1152], P('seq')
- d_tokens: bfloat16 [128, 17, 1152], P('seq')
- d_caption: float32 [4, 300, 1152], P(None, None, 'tp')
- d_condition: float32 [4, 1152], replicated
- d_w_qkv: float32 [1152, 3, 1152], P('seq', None, 'tp')
- d_w_out: float32 [1152, 1152], P('tp', 'seq')
- d_w_query2: float32 [1152, 1152], P('seq', 'tp')
- d_w_kv2: float32 [1152, 2, 1152], P('seq', None, 'tp')
- d_w_out2: float32 [1152, 1152], P('tp', 'seq')
- d_w_up: float32 [1152, 4608], P('seq', 'tp')
- d_w_down: float32 [4608, 1152], P('tp', 'seq')
- d_w_ada: float32 [1152, 6912], P('seq', 'tp')
Inputs may be any that keep to these rules, and one draw needn't show every extreme that they name: frames of each clip; they add up to 44 and one clip has 17. `cap_len`: live caption tokens of each clip, the first ones of its slots; they add up to 600 and one clip has 300.
All inputs are finite; a program needn't handle non-finite values.
Results may differ from a plain program's by a relative error of at most 0.024.
Values may be sent and summed in bfloat16 or wider, within the bound.
No kernel may reach another device: no remote copies, remote signals or barrier semaphores. Data moves between devices by JAX's collectives and lax.ppermute only.
A program may use at most 128 MiB of HBM per device.

v0:
```python
import jax
import jax.numpy as jnp
from jax import lax
from jax.sharding import PartitionSpec as P

HDIM = 72
CLIPS = 4
EPSILON = 1e-06
NEG_FILL = -1e30
HIGHEST = lax.Precision.HIGHEST


def normalize(rows):
    center = rows - jnp.mean(rows, -1, keepdims=True)
    return center * lax.rsqrt(jnp.mean(center * center, -1, keepdims=True) + EPSILON)


def modulate(rows, shift, scale):
    return normalize(rows) * (1.0 + scale[:, None, :]) + shift[:, None, :]


def total_rows(partial_value):
    return lax.psum(partial_value, "tp")


def frame_attention(triple, live, head_scale):
    raw = (
        jnp.einsum(
            "lfhe,lghe->lhfg", triple[:, :, 0], triple[:, :, 1], preferred_element_type=jnp.float32
        )
        * head_scale
    )
    probs = jax.nn.softmax(jnp.where(live[:, None, None, :], raw, NEG_FILL), axis=-1)
    result = jnp.einsum(
        "lhfg,lghe->lfhe",
        probs.astype(jnp.bfloat16),
        triple[:, :, 2],
        preferred_element_type=jnp.float32,
    )
    return (probs, result.astype(jnp.bfloat16))


def cross_scores(query, keys, clips, key_clip, key_live, head_scale):
    raw = jnp.einsum("rhe,khe->hrk", query, keys, preferred_element_type=jnp.float32) * head_scale
    allowed = (clips[:, None] == key_clip[None, :]) & key_live[None, :]
    return jnp.where(allowed[None], raw, NEG_FILL)


def shards(
    tokens,
    cotangent,
    caption,
    condition,
    frames,
    cap_len,
    clip_of,
    w_qkv,
    w_out,
    w_query2,
    w_kv2,
    w_out2,
    w_up,
    w_down,
    w_ada,
):
    seqs, fmax, width = tokens.shape
    row_count = seqs * fmax
    inner = w_qkv.shape[2]
    local_heads = inner // HDIM
    head_scale = HDIM ** (-0.5)
    full_qkv, full_out, full_query2, full_kv2, full_out2, full_up, full_down, full_ada = (
        lax.all_gather(w_qkv, "seq", axis=0, tiled=True),
        lax.all_gather(w_out, "seq", axis=1, tiled=True),
        lax.all_gather(w_query2, "seq", axis=0, tiled=True),
        lax.all_gather(w_kv2, "seq", axis=0, tiled=True),
        lax.all_gather(w_out2, "seq", axis=1, tiled=True),
        lax.all_gather(w_up, "seq", axis=0, tiled=True),
        lax.all_gather(w_down, "seq", axis=1, tiled=True),
        lax.all_gather(w_ada, "seq", axis=0, tiled=True),
    )
    qkv_matrix = full_qkv.reshape(width, 3 * inner)
    kv_matrix = full_kv2.reshape(width, 2 * inner)
    scaled = jax.nn.silu(condition).astype(jnp.bfloat16)
    mod_part = jnp.dot(scaled, full_ada, preferred_element_type=jnp.float32)
    mods = lax.all_gather(mod_part, "tp", axis=1, tiled=True).reshape(CLIPS, 6, width)
    clip_ids = jnp.arange(CLIPS)
    clip_hot = clip_of[:, None] == clip_ids[None, :]
    seq_mods = jnp.sum(jnp.where(clip_hot[:, :, None, None], mods[None], 0.0), 1)
    seq_frames = jnp.sum(jnp.where(clip_hot, frames[None, :], 0), 1)
    live = jnp.arange(fmax)[None, :] < seq_frames[:, None]
    own_live = live.astype(jnp.float32)[:, :, None]
    own_hot = clip_hot.astype(jnp.float32)
    key_count = caption.shape[0] * caption.shape[1]
    key_clip = jnp.arange(key_count) // caption.shape[1]
    key_len = jnp.sum(jnp.where(key_clip[:, None] == clip_ids[None, :], cap_len[None, :], 0), 1)
    key_live = jnp.arange(key_count) % caption.shape[1] < key_len
    row_clip = jnp.repeat(clip_of, fmax)
    block_seqs = min(32, seqs)
    blocks = seqs // block_seqs
    block_rows = block_seqs * fmax
    block_clip = row_clip.reshape(blocks, block_rows)
    own_input = tokens.astype(jnp.float32)
    attn_in = (
        modulate(own_input, seq_mods[:, 0], seq_mods[:, 1])
        .astype(jnp.bfloat16)
        .reshape(row_count, width)
    )
    triple = (
        jnp.dot(attn_in, qkv_matrix, preferred_element_type=jnp.float32)
        .astype(jnp.bfloat16)
        .reshape(seqs, fmax, 3, local_heads, HDIM)
    )
    probs, frame_out = frame_attention(triple, live, head_scale)
    frame_out = frame_out.reshape(row_count, inner)
    branch_one = total_rows(
        jnp.dot(frame_out, full_out, preferred_element_type=jnp.float32).reshape(seqs, fmax, width)
    )
    first = own_input + seq_mods[:, 2][:, None, :] * branch_one
    first_low = first.astype(jnp.bfloat16).reshape(row_count, width)
    cross_query = (
        jnp.dot(first_low, full_query2, preferred_element_type=jnp.float32)
        .astype(jnp.bfloat16)
        .reshape(blocks, block_rows, local_heads, HDIM)
    )
    cross_kv = (
        jnp.dot(caption.reshape(key_count, width), kv_matrix, preferred_element_type=jnp.float32)
        .astype(jnp.bfloat16)
        .reshape(key_count, 2, local_heads, HDIM)
    )
    cross_key = cross_kv[:, 0]
    cross_value = cross_kv[:, 1]

    def cross_block(pair):
        query, clips = pair
        scores = cross_scores(query, cross_key, clips, key_clip, key_live, head_scale)
        top = jnp.max(scores, -1, keepdims=True)
        weights = jnp.exp(scores - top)
        denom = jnp.sum(weights, -1, keepdims=True)
        block_out = jnp.einsum(
            "hrk,khe->rhe",
            (weights / denom).astype(jnp.bfloat16),
            cross_value,
            preferred_element_type=jnp.float32,
        )
        return (block_out.astype(jnp.bfloat16), (top + jnp.log(denom))[..., 0])

    cross_out, cross_lse = lax.map(cross_block, (cross_query, block_clip))
    cross_out = cross_out.reshape(row_count, inner)
    second = first + total_rows(
        jnp.dot(cross_out, full_out2, preferred_element_type=jnp.float32).reshape(seqs, fmax, width)
    )
    mlp_in = (
        modulate(second, seq_mods[:, 3], seq_mods[:, 4])
        .astype(jnp.bfloat16)
        .reshape(row_count, width)
    )
    hidden_pre = jnp.dot(mlp_in, full_up, preferred_element_type=jnp.float32)
    hidden = jax.nn.gelu(hidden_pre, approximate=True).astype(jnp.bfloat16)
    branch_three = total_rows(
        jnp.dot(hidden, full_down, preferred_element_type=jnp.float32).reshape(seqs, fmax, width)
    )
    third = second + seq_mods[:, 5][:, None, :] * branch_three
    output = (third * own_live).astype(jnp.bfloat16)
    grad_three = cotangent.astype(jnp.float32) * own_live
    d_branch3 = (
        (seq_mods[:, 5][:, None, :] * grad_three).astype(jnp.bfloat16).reshape(row_count, width)
    )
    grad_down = jnp.einsum("rk,rd->kd", hidden, d_branch3, preferred_element_type=jnp.float32)
    d_hidden = jnp.einsum("rd,kd->rk", d_branch3, full_down, preferred_element_type=jnp.float32)
    gelu_pull = jax.vjp(lambda value: jax.nn.gelu(value, approximate=True), hidden_pre)[1]
    d_pre = gelu_pull(d_hidden)[0].astype(jnp.bfloat16)
    grad_up = jnp.einsum("rd,rk->dk", mlp_in, d_pre, preferred_element_type=jnp.float32)
    d_mlp = total_rows(
        jnp.einsum("rk,dk->rd", d_pre, full_up, preferred_element_type=jnp.float32).reshape(
            seqs, fmax, width
        )
    )
    second_pull = jax.vjp(modulate, second, seq_mods[:, 3], seq_mods[:, 4])[1]
    norm_two, d_shift2, d_scale2 = second_pull(d_mlp)
    grad_two = grad_three + norm_two
    d_branch2 = grad_two.astype(jnp.bfloat16).reshape(row_count, width)
    grad_out2 = jnp.einsum("rc,rd->cd", cross_out, d_branch2, preferred_element_type=jnp.float32)
    d_cross = (
        jnp.einsum("rd,cd->rc", d_branch2, full_out2, preferred_element_type=jnp.float32)
        .astype(jnp.bfloat16)
        .reshape(blocks, block_rows, local_heads, HDIM)
    )

    def cross_back(carry, item):
        key_sum, value_sum = carry
        query, clips, block_lse, grad_block = item
        scores = cross_scores(query, cross_key, clips, key_clip, key_live, head_scale)
        weights = jnp.exp(scores - block_lse[..., None])
        value_sum = value_sum + jnp.einsum(
            "hrk,rhe->khe",
            weights.astype(jnp.bfloat16),
            grad_block,
            preferred_element_type=jnp.float32,
        )
        grad_weights = jnp.einsum(
            "rhe,khe->hrk", grad_block, cross_value, preferred_element_type=jnp.float32
        )
        grad_scores = (
            weights * (grad_weights - jnp.sum(weights * grad_weights, -1, keepdims=True))
        ).astype(jnp.bfloat16)
        grad_query = (
            jnp.einsum("hrk,khe->rhe", grad_scores, cross_key, preferred_element_type=jnp.float32)
            * head_scale
        ).astype(jnp.bfloat16)
        key_sum = (
            key_sum
            + jnp.einsum("hrk,rhe->khe", grad_scores, query, preferred_element_type=jnp.float32)
            * head_scale
        )
        return ((key_sum, value_sum), grad_query)

    zero_keys = jnp.zeros((key_count, local_heads, HDIM), jnp.float32)
    (key_grad, value_grad), d_query = lax.scan(
        cross_back, (zero_keys, zero_keys), (cross_query, block_clip, cross_lse, d_cross)
    )
    d_query = d_query.reshape(row_count, inner)
    grad_query2 = jnp.einsum("rd,rc->dc", first_low, d_query, preferred_element_type=jnp.float32)
    grad_one = grad_two + total_rows(
        jnp.einsum("rc,dc->rd", d_query, full_query2, preferred_element_type=jnp.float32).reshape(
            seqs, fmax, width
        )
    )
    d_branch1 = (
        (seq_mods[:, 2][:, None, :] * grad_one).astype(jnp.bfloat16).reshape(row_count, width)
    )
    grad_out = jnp.einsum("rc,rd->cd", frame_out, d_branch1, preferred_element_type=jnp.float32)
    d_frame = (
        jnp.einsum("rd,cd->rc", d_branch1, full_out, preferred_element_type=jnp.float32)
        .astype(jnp.bfloat16)
        .reshape(seqs, fmax, local_heads, HDIM)
    )
    d_value = jnp.einsum(
        "lhfg,lfhe->lghe", probs.astype(jnp.bfloat16), d_frame, preferred_element_type=jnp.float32
    )
    d_probs = jnp.einsum(
        "lfhe,lghe->lhfg", d_frame, triple[:, :, 2], preferred_element_type=jnp.float32
    )
    d_scores = (probs * (d_probs - jnp.sum(probs * d_probs, -1, keepdims=True))).astype(
        jnp.bfloat16
    )
    d_queries = (
        jnp.einsum("lhfg,lghe->lfhe", d_scores, triple[:, :, 1], preferred_element_type=jnp.float32)
        * head_scale
    )
    d_keys = (
        jnp.einsum("lhfg,lfhe->lghe", d_scores, triple[:, :, 0], preferred_element_type=jnp.float32)
        * head_scale
    )
    d_triple = (
        jnp.stack([d_queries, d_keys, d_value], 2)
        .astype(jnp.bfloat16)
        .reshape(row_count, 3 * inner)
    )
    grad_qkv = jnp.einsum(
        "rd,rc->dc", attn_in, d_triple, preferred_element_type=jnp.float32
    ).reshape(width, 3, inner)
    d_attn = total_rows(
        jnp.einsum("rc,dc->rd", d_triple, qkv_matrix, preferred_element_type=jnp.float32).reshape(
            seqs, fmax, width
        )
    )
    first_pull = jax.vjp(modulate, own_input, seq_mods[:, 0], seq_mods[:, 1])[1]
    norm_one, d_shift1, d_scale1 = first_pull(d_attn)
    d_tokens = (grad_one + norm_one).astype(jnp.bfloat16)
    d_gate1 = jnp.sum(grad_one * branch_one, 1)
    d_gate2 = jnp.sum(grad_three * branch_three, 1)
    seq_terms = jnp.stack([d_shift1, d_scale1, d_gate1, d_shift2, d_scale2, d_gate2], 1)
    d_mods = jnp.einsum("lc,ljd->cjd", own_hot, seq_terms, precision=HIGHEST).reshape(
        CLIPS, 6 * width
    )
    kv_grad = jnp.stack([key_grad, value_grad], 1)
    kv_total, mods_total = (
        lax.psum(kv_grad.astype(jnp.bfloat16), "seq").astype(jnp.float32),
        lax.psum(d_mods.astype(jnp.bfloat16), "seq").astype(jnp.float32),
    )
    col_count = mods_total.shape[1] // lax.axis_size("tp")
    mod_cols = lax.dynamic_slice_in_dim(mods_total, lax.axis_index("tp") * col_count, col_count, 1)
    seq_rows = w_ada.shape[0]
    seq_start = lax.axis_index("seq") * seq_rows
    scaled_rows = lax.dynamic_slice_in_dim(scaled, seq_start, seq_rows, 1).astype(jnp.float32)
    grad_ada = jnp.einsum("cd,ck->dk", scaled_rows, mod_cols, precision=HIGHEST)
    silu_pull = jax.vjp(jax.nn.silu, condition)[1]
    cond_part = silu_pull(
        jnp.einsum("ck,dk->cd", mod_cols, full_ada.astype(jnp.float32), precision=HIGHEST)
    )[0]
    d_condition = lax.psum(cond_part, "tp")
    kv_low = kv_total.astype(jnp.bfloat16).reshape(key_count, 2 * inner)
    caption_rows = lax.dynamic_slice_in_dim(
        caption.reshape(key_count, width), seq_start, seq_rows, 1
    )
    grad_kv2 = jnp.einsum(
        "kd,kc->dc", caption_rows, kv_low, preferred_element_type=jnp.float32
    ).reshape(seq_rows, 2, inner)
    caption_part = jnp.einsum(
        "kc,dc->kd", kv_low, kv_matrix, preferred_element_type=jnp.float32
    ).reshape(caption.shape)
    d_caption = lax.psum_scatter(
        caption_part.astype(jnp.bfloat16), "tp", scatter_dimension=2, tiled=True
    ).astype(jnp.float32)
    summed = (
        lax.psum_scatter(
            grad_qkv.astype(jnp.bfloat16), "seq", scatter_dimension=0, tiled=True
        ).astype(jnp.float32),
        lax.psum_scatter(
            grad_out.astype(jnp.bfloat16), "seq", scatter_dimension=1, tiled=True
        ).astype(jnp.float32),
        lax.psum_scatter(
            grad_query2.astype(jnp.bfloat16), "seq", scatter_dimension=0, tiled=True
        ).astype(jnp.float32),
        lax.psum_scatter(
            grad_out2.astype(jnp.bfloat16), "seq", scatter_dimension=1, tiled=True
        ).astype(jnp.float32),
        lax.psum_scatter(
            grad_up.astype(jnp.bfloat16), "seq", scatter_dimension=0, tiled=True
        ).astype(jnp.float32),
        lax.psum_scatter(
            grad_down.astype(jnp.bfloat16), "seq", scatter_dimension=1, tiled=True
        ).astype(jnp.float32),
    )
    return (
        output,
        d_tokens,
        d_caption,
        d_condition,
        summed[0],
        summed[1],
        summed[2],
        grad_kv2,
        summed[3],
        summed[4],
        summed[5],
        grad_ada,
    )


def solution(mesh):
    return jax.shard_map(
        shards,
        mesh=mesh,
        in_specs=(
            P("seq", None, None),
            P("seq", None, None),
            P(),
            P(),
            P(),
            P(),
            P("seq"),
            P("seq", None, "tp"),
            P("tp", "seq"),
            P("seq", "tp"),
            P("seq", None, "tp"),
            P("tp", "seq"),
            P("seq", "tp"),
            P("tp", "seq"),
            P("seq", "tp"),
        ),
        out_specs=(
            P("seq", None, None),
            P("seq", None, None),
            P(None, None, "tp"),
            P(),
            P("seq", None, "tp"),
            P("tp", "seq"),
            P("seq", "tp"),
            P("seq", None, "tp"),
            P("tp", "seq"),
            P("seq", "tp"),
            P("tp", "seq"),
            P("seq", "tp"),
        ),
        check_vma=False,
    )
```

profile of v0, /device:TPU:0, one launch (start us, length us, event | category | flops | bytes accessed | tf_op | source)
XLA Modules:
  0.0 1068.3 jit_solution(13612882484881826433)
XLA Ops:
  14.8 15.0 %all_gather.30 = bf16[288,1152]{0,1:T(8,128)(2,1)S(1)} all-gather(bf16[288,144]{0,1:T(8,128)(2,1)S(1)} %copy-done.45), channel_id=1, replica_groups=mesh['seq'=8,'tp'=4] {'seq'}, dimensions={1}, use_global_device_ids=true | all-gather | bytes 746496 | tf_op jit(solution)/shard_map/all_gather | solution.py:73
  29.7 13.7 %all_gather.32 = bf16[1152,288]{1,0:T(8,128)(2,1)S(1)} all-gather(bf16[144,288]{1,0:T(8,128)(2,1)S(1)} %copy-done.46), channel_id=1, replica_groups=mesh['seq'=8,'tp'=4] {'seq'}, dimensions={0}, use_global_device_ids=true | all-gather | bytes 746496 | tf_op jit(solution)/shard_map/all_gather | solution.py:74
  43.4 11.3 %all_gather.33 = bf16[288,1152]{0,1:T(8,128)(2,1)} all-gather(bf16[288,144]{0,1:T(8,128)(2,1)S(1)} %copy-done.47), channel_id=1, replica_groups=mesh['seq'=8,'tp'=4] {'seq'}, dimensions={1}, use_global_device_ids=true | all-gather | bytes 746496 | tf_op jit(solution)/shard_map/all_gather | solution.py:76
  64.2 21.8 %all-gather.7.cloned.1.call-done = bf16[1152,1728]{1,0:T(8,128)(2,1)} async-done(((bf16[144,1728]{1,0:T(8,128)(2,1)}), bf16[1152,1728]{1,0:T(8,128)(2,1)}) %all-gather.7.cloned.1.call-update) | async-done | bytes 3981328 | tf_op jit(solution)/shard_map/all_gather | solution.py:79
  88.8 13.4 %all-gather = f32[4,1728,4]{1,2,0:T(4,128)S(1)} all-gather(f32[1,1728,4]{1,2,0:T(4,128)S(1)} %convolution_bitcast_fusion), channel_id=1, replica_groups=mesh['seq'=8,'tp'=4] {'tp'}, dimensions={0}, use_global_device_ids=true | all-gather | bytes 138240 | tf_op jit(solution)/shard_map/all_gather | solution.py:85
  123.3 5.6 copy.152
  128.9 5.6 convolution_convert_fusion.4
  134.5 63.4 %all-reduce.8.cloned.1.call-done = f32[16,17,1152]{2,1,0:T(8,128)} async-done(((f32[16,17,1152]{2,1,0:T(8,128)}), f32[16,17,1152]{2,1,0:T(8,128)}) %all-reduce.8.cloned.1.call-update) | async-done | bytes 1253392 | tf_op jit(solution)/shard_map/psum | solution.py:23
  212.2 73.3 %all-reduce.10.cloned.1.call-done = f32[16,17,1152]{2,1,0:T(8,128)} async-done(((f32[16,17,1152]{2,1,0:T(8,128)}), f32[16,17,1152]{2,1,0:T(8,128)}) %all-reduce.10.cloned.1.call-update) | async-done | bytes 1253392 | tf_op jit(solution)/shard_map/psum | solution.py:23
  295.4 21.2 %all-gather.15.cloned.1.call-done = bf16[1152,1152]{0,1:T(8,128)(2,1)} async-done(((bf16[1152,144]{0,1:T(8,128)(2,1)}), bf16[1152,1152]{0,1:T(8,128)(2,1)}) %all-gather.15.cloned.1.call-update) | async-done | bytes 2654224 | tf_op jit(solution)/shard_map/all_gather | solution.py:78
  320.7 28.1 %all-gather.13.cloned.1.call-done = bf16[1152,1152]{1,0:T(8,128)(2,1)} async-done(((bf16[144,1152]{1,0:T(8,128)(2,1)}), bf16[1152,1152]{1,0:T(8,128)(2,1)}) %all-gather.13.cloned.1.call-update) | async-done | bytes 2654224 | tf_op jit(solution)/shard_map/all_gather | solution.py:77
  348.8 5.0 fusion.36
  359.8 75.4 %all-reduce.12.cloned.1.call-done = f32[16,17,1152]{2,1,0:T(8,128)} async-done(((f32[16,17,1152]{2,1,0:T(8,128)}), f32[16,17,1152]{2,1,0:T(8,128)}) %all-reduce.12.cloned.1.call-update) | async-done | bytes 1253392 | tf_op jit(solution)/shard_map/psum | solution.py:23
  476.0 59.8 %all-reduce.14.cloned.1.call-done = f32[16,17,1152]{2,1,0:T(8,128)} async-done(((f32[16,17,1152]{2,1,0:T(8,128)}), f32[16,17,1152]{2,1,0:T(8,128)}) %all-reduce.14.cloned.1.call-update) | async-done | bytes 1253392 | tf_op jit(solution)/shard_map/psum | solution.py:23
  604.5 6.6 convolution_convert_fusion.2
  611.1 23.5 %reduce-scatter.16.cloned.1.call-done = bf16[288,144]{0,1:T(8,128)(2,1)} async-done(((bf16[288,1152]{0,1:T(8,128)(2,1)}), bf16[288,144]{0,1:T(8,128)(2,1)}) %reduce-scatter.16.cloned.1.call-update) | async-done | bytes 82960 | tf_op jit(solution)/shard_map/reduce_scatter | solution.py:315
  636.2 36.7 %reduce-scatter.14.cloned.1.call-done = bf16[144,288]{1,0:T(8,128)(2,1)} async-done(((bf16[1152,288]{1,0:T(8,128)(2,1)}), bf16[144,288]{1,0:T(8,128)(2,1)}) %reduce-scatter.14.cloned.1.call-update) | async-done | bytes 82960 | tf_op jit(solution)/shard_map/reduce_scatter | solution.py:312
  674.4 37.7 %reduce-scatter.12.cloned.1.call-done = bf16[288,144]{0,1:T(8,128)(2,1)} async-done(((bf16[288,1152]{0,1:T(8,128)(2,1)}), bf16[288,144]{0,1:T(8,128)(2,1)}) %reduce-scatter.12.cloned.1.call-update) | async-done | bytes 82960 | tf_op jit(solution)/shard_map/reduce_scatter | solution.py:309
  713.7 45.6 %reduce-scatter.18.cloned.1.call-done = bf16[144,1152]{1,0:T(8,128)(2,1)} async-done(((bf16[1152,1152]{1,0:T(8,128)(2,1)}), bf16[144,1152]{1,0:T(8,128)(2,1)}) %reduce-scatter.18.cloned.1.call-update) | async-done | bytes 331792 | tf_op jit(solution)/shard_map/reduce_scatter | solution.py:318
  761.2 45.7 %reduce-scatter.20.cloned.1.call-done = bf16[1152,144]{0,1:T(8,128)(2,1)} async-done(((bf16[1152,1152]{0,1:T(8,128)(2,1)}), bf16[1152,144]{0,1:T(8,128)(2,1)}) %reduce-scatter.20.cloned.1.call-update) | async-done | bytes 331792 | tf_op jit(solution)/shard_map/reduce_scatter | solution.py:321
  808.7 135.2 %all-reduce.18.cloned.1.call-done = (f32[16,17,1152]{2,1,0:T(8,128)}, f32[16,17,1152]{2,1,0:T(8,128)}) async-done(((f32[16,17,1152]{2,1,0:T(8,128)}, f32[16,17,1152]{2,1,0:T(8,128)}), (f32[16,17,1152]{2,1,0:T(8,128)}, f32[16,17,1152]{2,1,0:T(8,128)})) %all-reduce.18.cloned.1.call-update) | async-done | bytes 2506768 | tf_op jit(solution)/shard_map/psum | solution.py:23
  951.2 24.9 %psum.70 = bf16[4,6912]{1,0:T(4,128)(2,1)S(1)} all-reduce(bf16[4,6912]{1,0:T(4,128)(2,1)S(1)} %bitcast.198), channel_id=1, replica_groups=mesh['seq'=8,'tp'=4] {'seq'}, use_global_device_ids=true, to_apply=%region_31.32 | all-reduce | flops 27648 | bytes 110592 | tf_op jit(solution)/shard_map/psum | solution.py:279
  979.5 17.6 %psum.71 = f32[4,1152]{1,0:T(4,128)} all-reduce(f32[4,1152]{1,0:T(4,128)S(1)} %fusion.68), channel_id=1, replica_groups=mesh['seq'=8,'tp'=4] {'tp'}, use_global_device_ids=true, to_apply=%region_32.33 | all-reduce | flops 4608 | bytes 36864 | tf_op jit(solution)/shard_map/psum | solution.py:291
  1001.1 57.7 %reduce-scatter.8.cloned.1.call-done = bf16[4,300,288]{1,2,0:T(8,128)(2,1)} async-done(((bf16[4,300,1152]{1,2,0:T(8,128)(2,1)}), bf16[4,300,288]{1,2,0:T(8,128)(2,1)}) %reduce-scatter.8.cloned.1.call-update) | async-done | bytes 691216 | tf_op jit(solution)/shard_map/reduce_scatter | solution.py:302
  (301 shorter events, 209.3 us)
Async XLA Ops:
  7.2 52.7 %all-gather.9.cloned.1.call-start = ((), (), s32[]{:S(2)}) async-start(), calls=%async_computation.8 | async-start | bytes 2985984 | tf_op jit(solution)/shard_map/all_gather | solution.py:72
  8.0 78.0 %all-gather.7.cloned.1.call-start = ((), (), s32[]{:S(2)}) async-start(), calls=%async_computation.7 | async-start | bytes 4644864 | tf_op jit(solution)/shard_map/all_gather | solution.py:79
  8.7 114.6 %all-gather.11.cloned.1.call-start = ((), (), s32[]{:S(2)}) async-start(), calls=%async_computation.10 | async-start | bytes 1990656 | tf_op jit(solution)/shard_map/all_gather | solution.py:75
  9.5 188.4 %all-reduce.8.cloned.1.call-start = ((), (), s32[]{:S(2)}) async-start(), calls=%async_computation.9 | async-start | bytes 3538944 | tf_op jit(solution)/shard_map/psum | solution.py:23
  29.7 90.2 %copy-start.9 = (bf16[288,1152]{0,1:T(8,128)(2,1)}, bf16[288,1152]{0,1:T(8,128)(2,1)S(1)}, u32[]{:S(2)}) copy-start(bf16[288,1152]{0,1:T(8,128)(2,1)S(1)} %all_gather.30) | copy-start | bytes 1990660
  43.4 156.5 %copy-start.10 = (bf16[1152,288]{1,0:T(8,128)(2,1)}, bf16[1152,288]{1,0:T(8,128)(2,1)S(1)}, u32[]{:S(2)}) copy-start(bf16[1152,288]{1,0:T(8,128)(2,1)S(1)} %all_gather.32) | copy-start | bytes 1990660
  103.3 182.3 %copy-start.31 = (f32[16,1152]{1,0:T(8,128)}, f32[16,1152]{1,0:T(8,128)S(1)}, u32[]{:S(2)}) copy-start(f32[16,1152]{1,0:T(8,128)S(1)} %get-tuple-element.159) | copy-start | bytes 221188
  103.3 185.1 %copy-start.36 = (f32[16,1152]{1,0:T(8,128)}, f32[16,1152]{1,0:T(8,128)S(1)}, u32[]{:S(2)}) copy-start(f32[16,1152]{1,0:T(8,128)S(1)} %get-tuple-element.154) | copy-start | bytes 221188
  121.9 163.6 %all-reduce.10.cloned.1.call-start = ((), (), s32[]{:S(2)}) async-start(), calls=%async_computation.11 | async-start | bytes 3538944 | tf_op jit(solution)/shard_map/psum | solution.py:23
  210.8 105.8 %all-gather.15.cloned.1.call-start = ((), (), s32[]{:S(2)}) async-start(), calls=%async_computation.13 | async-start | bytes 2985984 | tf_op jit(solution)/shard_map/all_gather | solution.py:78
  211.4 137.4 %all-gather.13.cloned.1.call-start = ((), (), s32[]{:S(2)}) async-start(), calls=%async_computation.12 | async-start | bytes 2985984 | tf_op jit(solution)/shard_map/all_gather | solution.py:77
  212.2 223.0 %all-reduce.12.cloned.1.call-start = ((), (), s32[]{:S(2)}) async-start(), calls=%async_computation.14 | async-start | bytes 3538944 | tf_op jit(solution)/shard_map/psum | solution.py:23
  359.5 176.3 %all-reduce.14.cloned.1.call-start = ((), (), s32[]{:S(2)}) async-start(), calls=%async_computation.15 | async-start | bytes 3538944 | tf_op jit(solution)/shard_map/psum | solution.py:23
  461.1 135.5 %all-reduce.16.cloned.1.call-start = ((), (), s32[]{:S(2)}) async-start(), calls=%async_computation.16 | async-start | bytes 2949120 | tf_op jit(solution)/shard_map/psum | solution.py:278
  469.2 165.4 %reduce-scatter.16.cloned.1.call-start = ((), (), s32[]{:S(2)}) async-start(), calls=%async_computation.21 | async-start | bytes 995328 | tf_op jit(solution)/shard_map/reduce_scatter | solution.py:315
  472.2 200.7 %reduce-scatter.14.cloned.1.call-start = ((), (), s32[]{:S(2)}) async-start(), calls=%async_computation.20 | async-start | bytes 995328 | tf_op jit(solution)/shard_map/reduce_scatter | solution.py:312
  476.0 236.2 %reduce-scatter.12.cloned.1.call-start = ((), (), s32[]{:S(2)}) async-start(), calls=%async_computation.19 | async-start | bytes 995328 | tf_op jit(solution)/shard_map/reduce_scatter | solution.py:309
  547.0 212.3 %reduce-scatter.18.cloned.1.call-start = ((), (), s32[]{:S(2)}) async-start(), calls=%async_computation.22 | async-start | bytes 2985984 | tf_op jit(solution)/shard_map/reduce_scatter | solution.py:318
  551.9 254.9 %reduce-scatter.20.cloned.1.call-start = ((), (), s32[]{:S(2)}) async-start(), calls=%async_computation.23 | async-start | bytes 2985984 | tf_op jit(solution)/shard_map/reduce_scatter | solution.py:321
  556.7 387.1 %all-reduce.18.cloned.1.call-start = ((), (), s32[]{:S(2)}) async-start(), calls=%async_computation.24 | async-start | bytes 7077888 | tf_op jit(solution)/shard_map/psum | solution.py:23
  581.9 417.3 %reduce-scatter.10.cloned.1.call-start = ((), (), s32[]{:S(2)}) async-start(), calls=%async_computation.18 | async-start | bytes 2985984 | tf_op jit(solution)/shard_map/reduce_scatter | solution.py:306
  591.9 466.9 %reduce-scatter.8.cloned.1.call-start = ((), (), s32[]{:S(2)}) async-start(), calls=%async_computation.17 | async-start | bytes 4423680 | tf_op jit(solution)/shard_map/reduce_scatter | solution.py:302
  611.1 332.8 %copy-start.23 = (f32[16,1152]{1,0:T(8,128)S(1)}, f32[16,1152]{1,0:T(8,128)}, u32[]{:S(2)}) copy-start(f32[16,1152]{1,0:T(8,128)} %copy-done.22) | copy-start | bytes 221188
  761.2 184.8 %copy-start.51 = (f32[16,17]{1,0:T(8,128)S(1)}, f32[16,17]{1,0:T(8,128)}, u32[]{:S(2)}) copy-start(f32[16,17]{1,0:T(8,128)} %copy-done.50) | copy-start | bytes 3268
  (60 other events, 465.9 us)
Sparse Core Ops, SparseCore 0:
  10.0 37.6 all-gather.8
  49.5 36.4 all-gather.6
  87.9 26.5 all-gather.10
  122.0 75.7 all-reduce.7
  211.0 74.5 all-reduce.9
  287.3 29.2 all-gather.14
  318.5 30.2 all-gather.12
  359.6 75.5 all-reduce.11
  461.2 74.5 all-reduce.13
  538.9 57.6 all-reduce.15
  600.2 34.3 reduce-scatter.15
  637.7 35.1 reduce-scatter.13
  677.0 35.0 reduce-scatter.11
  715.5 43.7 reduce-scatter.17
  763.0 43.7 reduce-scatter.19
  809.7 134.1 all-reduce.17
  947.2 42.9 reduce-scatter.9
  992.4 66.3 reduce-scatter.7
where the time goes:
time: 1080 us; the launch traced here: 1070 us
  waiting for transfers between devices  733 us (68%)
  matrix products  105 us (10%)
  blocking collectives  95.8 us (9%)
  local copies, waits for them, and re-layouts  71.9 us (7%)
  other arithmetic  45.7 us (4%)
  between operations  15.4 us (1%)
    psum x5, waiting for transfers between devices, total_rows(): return lax.psum(partial_value, 'tp')  407 us
    reduce_scatter x1, waiting for transfers between devices, shards(): lax.psum_scatter(caption_part.astype(jnp.bfloat16), 'tp', scatter_dimensi...  57.7 us
    reduce_scatter x1, waiting for transfers between devices, shards(): lax.psum_scatter(grad_down.astype(jnp.bfloat16), 'seq', scatter_dimension...  45.7 us
    reduce_scatter x1, waiting for transfers between devices, shards(): lax.psum_scatter(grad_up.astype(jnp.bfloat16), 'seq', scatter_dimension=0...  45.6 us
    reduce_scatter x1, waiting for transfers between devices, shards(): lax.psum_scatter(grad_out.astype(jnp.bfloat16), 'seq', scatter_dimension=...  37.7 us
    reduce_scatter x1, waiting for transfers between devices, shards(): lax.psum_scatter(grad_query2.astype(jnp.bfloat16), 'seq', scatter_dimensi...  36.7 us
    all_gather x1, waiting for transfers between devices, shards(): lax.all_gather(w_up, 'seq', axis=0, tiled=True)  28.1 us
    psum x1, blocking collectives, shards(): lax.psum(d_mods.astype(jnp.bfloat16), 'seq').astype(jnp.float32)  24.9 us
  transfers between devices with their start and end apart: 18, of which 15 were waited for; matrix products, arithmetic and copies ran while one was open for 15% of the time, Pallas kernels for 0%

commit v1 on v0

--- a/solution.py
+++ b/solution.py
@@ -8,6 +8,23 @@
 EPSILON = 1e-06
 NEG_FILL = -1e30
 HIGHEST = lax.Precision.HIGHEST
+
+
+def _turn_strips_all(chunk, on_dim=0):
+    mesh_dim = "seq"
+    cores_n = lax.axis_size(mesh_dim)
+    made = list(map(lambda t: (t, (t + 1) % cores_n), range(cores_n)))
+    pieces_in = list(map(lambda t: (t, (t - 1) % cores_n), range(cores_n)))
+    wide_out, carry_out = ([chunk], [chunk])
+    for _ in range(cores_n // 2):
+        wide_out.append(lax.ppermute(wide_out[-1], mesh_dim, perm=made))
+    for _ in [*range((cores_n - 1) // 2)]:
+        carry_out.append(lax.ppermute(carry_out[-1], mesh_dim, pieces_in))
+    far_arr = jnp.concatenate([*wide_out[::-1], *carry_out[1:]], axis=on_dim)
+    everything = jnp.roll(
+        far_arr, (lax.axis_index(mesh_dim) - cores_n // 2) * chunk.shape[on_dim], axis=on_dim
+    )
+    return everything
 
 
 def normalize(rows):
@@ -74,7 +91,7 @@
         lax.all_gather(w_query2, "seq", axis=0, tiled=True),
         lax.all_gather(w_kv2, "seq", axis=0, tiled=True),
         lax.all_gather(w_out2, "seq", axis=1, tiled=True),
-        lax.all_gather(w_up, "seq", axis=0, tiled=True),
+        _turn_strips_all(w_up),
         lax.all_gather(w_down, "seq", axis=1, tiled=True),
         lax.all_gather(w_ada, "seq", axis=0, tiled=True),
     )

time: 1080 us -> 1040 us (0.963)
  waiting for transfers between devices: 733 us -> 671 us
  local copies, waits for them, and re-layouts: 71.9 us -> 86.7 us
    psum x5, waiting for transfers between devices: 407 us -> 344 us  [total_rows(): return lax.psum(partial_value, 'tp')]
    all_gather x1 -> x0, waiting for transfers between devices: 28.1 us -> none  [shards(): lax.all_gather(w_up, 'seq', axis=0, tiled=True)]
    ppermute x0 -> x7, waiting for transfers between devices: none -> 21.5 us  [the longest x4 21.5 us: _turn_strips_all(): wide_out.append(lax.ppermute(wide_out[-1], mesh_dim, perm=made))]
    all_gather x1, waiting for transfers between devices: 21.2 us -> 0.59 us  [shards(): lax.all_gather(w_down, 'seq', axis=1, tiled=True)]
    unnamed x142 -> x149, local copies, waits for them, and re-layouts: 15.6 us -> 34.4 us
    all_gather x1, waiting for transfers between devices: 0.01 us -> 16.8 us  [shards(): lax.all_gather(w_qkv, 'seq', axis=0, tiled=True)]
    all_gather x1, waiting for transfers between devices: 21.8 us -> 34.1 us  [shards(): lax.all_gather(w_ada, 'seq', axis=0, tiled=True)]
  transfers between devices with their start and end apart: 18 -> 24, of which waited for: 15 -> 17; matrix products, arithmetic and copies ran while one was open for 15% -> 18% of each run, Pallas kernels for 0% -> 0%
where the time goes in v1:
time: 1040 us; the launch traced here: 1030 us
  waiting for transfers between devices  671 us (65%)
  matrix products  105 us (10%)
  blocking collectives  92.8 us (9%)
  local copies, waits for them, and re-layouts  86.7 us (8%)
  other arithmetic  46.6 us (4%)
  between operations  15.1 us (1%)
    psum x5, waiting for transfers between devices, total_rows(): return lax.psum(partial_value, 'tp')  344 us
    reduce_scatter x1, waiting for transfers between devices, shards(): lax.psum_scatter(caption_part.astype(jnp.bfloat16), 'tp', scatter_dimensi...  57.7 us
    reduce_scatter x1, waiting for transfers between devices, shards(): lax.psum_scatter(grad_up.astype(jnp.bfloat16), 'seq', scatter_dimension=0...  45.7 us
    reduce_scatter x1, waiting for transfers between devices, shards(): lax.psum_scatter(grad_down.astype(jnp.bfloat16), 'seq', scatter_dimension...  45.7 us
    reduce_scatter x1, waiting for transfers between devices, shards(): lax.psum_scatter(grad_out.astype(jnp.bfloat16), 'seq', scatter_dimension=...  37.5 us
    reduce_scatter x1, waiting for transfers between devices, shards(): lax.psum_scatter(grad_query2.astype(jnp.bfloat16), 'seq', scatter_dimensi...  36.8 us
    unnamed x149, local copies, waits for them, and re-layouts  34.4 us
    all_gather x1, waiting for transfers between devices, shards(): lax.all_gather(w_ada, 'seq', axis=0, tiled=True)  34.1 us
  transfers between devices with their start and end apart: 24, of which 17 were waited for; matrix products, arithmetic and copies ran while one was open for 18% of the time, Pallas kernels for 0%

profile of v1, /device:TPU:0, one launch (start us, length us, event | category | flops | bytes accessed | tf_op | source)
XLA Modules:
  0.0 1026.7 jit_solution(6933198774202900546)
XLA Ops:
  13.4 14.2 %all_gather.27 = bf16[288,1152]{0,1:T(8,128)(2,1)S(1)} all-gather(bf16[288,144]{0,1:T(8,128)(2,1)S(1)} %copy-done.48), channel_id=1, replica_groups=mesh['seq'=8,'tp'=4] {'seq'}, dimensions={1}, use_global_device_ids=true | all-gather | bytes 746496 | tf_op jit(solution)/shard_map/all_gather | solution.py:90
  27.6 16.8 %all-gather.8.cloned.1.call-done = bf16[1152,3,288]{2,0,1:T(8,128)(2,1)} async-done(((bf16[144,3,288]{2,0,1:T(8,128)(2,1)}), bf16[1152,3,288]{2,0,1:T(8,128)(2,1)}) %all-gather.8.cloned.1.call-update) | async-done | bytes 1990672 | tf_op jit(solution)/shard_map/all_gather | solution.py:89
  48.7 34.1 %all-gather.6.cloned.1.call-done = bf16[1152,1728]{1,0:T(8,128)(2,1)} async-done(((bf16[144,1728]{1,0:T(8,128)(2,1)}), bf16[1152,1728]{1,0:T(8,128)(2,1)}) %all-gather.6.cloned.1.call-update) | async-done | bytes 3981328 | tf_op jit(solution)/shard_map/all_gather | solution.py:96
  85.6 13.4 %all-gather = f32[4,1728,4]{1,2,0:T(4,128)S(1)} all-gather(f32[1,1728,4]{1,2,0:T(4,128)S(1)} %convolution_bitcast_fusion), channel_id=1, replica_groups=mesh['seq'=8,'tp'=4] {'tp'}, dimensions={0}, use_global_device_ids=true | all-gather | bytes 138240 | tf_op jit(solution)/shard_map/all_gather | solution.py:102
  116.1 7.8 collective-permute-done
  128.1 12.1 %all_gather.29 = bf16[1152,288]{1,0:T(8,128)(2,1)S(1)} all-gather(bf16[144,288]{1,0:T(8,128)(2,1)} %param.24), channel_id=1, replica_groups=mesh['seq'=8,'tp'=4] {'seq'}, dimensions={0}, use_global_device_ids=true | all-gather | bytes 746496 | tf_op jit(solution)/shard_map/all_gather | solution.py:91
  140.1 10.6 %all_gather.30 = bf16[288,1152]{0,1:T(8,128)(2,1)S(1)} all-gather(bf16[288,144]{0,1:T(8,128)(2,1)} %param.26), channel_id=1, replica_groups=mesh['seq'=8,'tp'=4] {'seq'}, dimensions={1}, use_global_device_ids=true | all-gather | bytes 746496 | tf_op jit(solution)/shard_map/all_gather | solution.py:93
  153.6 7.3 collective-permute-done.2
  164.7 6.4 collective-permute-done.3
  189.6 6.6 copy.152
  196.2 5.6 convolution_convert_fusion.4
  224.8 74.6 %all-reduce.10.cloned.1.call-done = f32[16,17,1152]{2,1,0:T(8,128)} async-done(((f32[16,17,1152]{2,1,0:T(8,128)}), f32[16,17,1152]{2,1,0:T(8,128)}) %all-reduce.10.cloned.1.call-update) | async-done | bytes 1253392 | tf_op jit(solution)/shard_map/psum | solution.py:40
  319.4 74.4 %all-reduce.12.cloned.1.call-done = f32[16,17,1152]{2,1,0:T(8,128)} async-done(((f32[16,17,1152]{2,1,0:T(8,128)}), f32[16,17,1152]{2,1,0:T(8,128)}) %all-reduce.12.cloned.1.call-update) | async-done | bytes 1253392 | tf_op jit(solution)/shard_map/psum | solution.py:40
  434.7 59.8 %all-reduce.14.cloned.1.call-done = f32[16,17,1152]{2,1,0:T(8,128)} async-done(((f32[16,17,1152]{2,1,0:T(8,128)}), f32[16,17,1152]{2,1,0:T(8,128)}) %all-reduce.14.cloned.1.call-update) | async-done | bytes 1253392 | tf_op jit(solution)/shard_map/psum | solution.py:40
  563.3 6.6 convolution_convert_fusion.2
  569.9 23.4 %reduce-scatter.16.cloned.1.call-done = bf16[288,144]{0,1:T(8,128)(2,1)} async-done(((bf16[288,1152]{0,1:T(8,128)(2,1)}), bf16[288,144]{0,1:T(8,128)(2,1)}) %reduce-scatter.16.cloned.1.call-update) | async-done | bytes 82960 | tf_op jit(solution)/shard_map/reduce_scatter | solution.py:332
  594.9 36.8 %reduce-scatter.14.cloned.1.call-done = bf16[144,288]{1,0:T(8,128)(2,1)} async-done(((bf16[1152,288]{1,0:T(8,128)(2,1)}), bf16[144,288]{1,0:T(8,128)(2,1)}) %reduce-scatter.14.cloned.1.call-update) | async-done | bytes 82960 | tf_op jit(solution)/shard_map/reduce_scatter | solution.py:329
  633.3 37.5 %reduce-scatter.12.cloned.1.call-done = bf16[288,144]{0,1:T(8,128)(2,1)} async-done(((bf16[288,1152]{0,1:T(8,128)(2,1)}), bf16[288,144]{0,1:T(8,128)(2,1)}) %reduce-scatter.12.cloned.1.call-update) | async-done | bytes 82960 | tf_op jit(solution)/shard_map/reduce_scatter | solution.py:326
  672.3 45.7 %reduce-scatter.18.cloned.1.call-done = bf16[144,1152]{1,0:T(8,128)(2,1)} async-done(((bf16[1152,1152]{1,0:T(8,128)(2,1)}), bf16[144,1152]{1,0:T(8,128)(2,1)}) %reduce-scatter.18.cloned.1.call-update) | async-done | bytes 331792 | tf_op jit(solution)/shard_map/reduce_scatter | solution.py:335
  719.9 45.7 %reduce-scatter.20.cloned.1.call-done = bf16[1152,144]{0,1:T(8,128)(2,1)} async-done(((bf16[1152,1152]{0,1:T(8,128)(2,1)}), bf16[1152,144]{0,1:T(8,128)(2,1)}) %reduce-scatter.20.cloned.1.call-update) | async-done | bytes 331792 | tf_op jit(solution)/shard_map/reduce_scatter | solution.py:338
  767.4 135.2 %all-reduce.18.cloned.1.call-done = (f32[16,17,1152]{2,1,0:T(8,128)}, f32[16,17,1152]{2,1,0:T(8,128)}) async-done(((f32[16,17,1152]{2,1,0:T(8,128)}, f32[16,17,1152]{2,1,0:T(8,128)}), (f32[16,17,1152]{2,1,0:T(8,128)}, f32[16,17,1152]{2,1,0:T(8,128)})) %all-reduce.18.cloned.1.call-update) | async-done | bytes 2506768 | tf_op jit(solution)/shard_map/psum | solution.py:40
  910.0 24.9 %psum.70 = bf16[4,6912]{1,0:T(4,128)(2,1)S(1)} all-reduce(bf16[4,6912]{1,0:T(4,128)(2,1)S(1)} %bitcast.194), channel_id=1, replica_groups=mesh['seq'=8,'tp'=4] {'seq'}, use_global_device_ids=true, to_apply=%region_31.32 | all-reduce | flops 27648 | bytes 110592 | tf_op jit(solution)/shard_map/psum | solution.py:296
  938.2 17.6 %psum.71 = f32[4,1152]{1,0:T(4,128)} all-reduce(f32[4,1152]{1,0:T(4,128)S(1)} %fusion.72), channel_id=1, replica_groups=mesh['seq'=8,'tp'=4] {'tp'}, use_global_device_ids=true, to_apply=%region_32.33 | all-reduce | flops 4608 | bytes 36864 | tf_op jit(solution)/shard_map/psum | solution.py:308
  959.8 57.7 %reduce-scatter.8.cloned.1.call-done = bf16[4,300,288]{1,2,0:T(8,128)(2,1)} async-done(((bf16[4,300,1152]{1,2,0:T(8,128)(2,1)}), bf16[4,300,288]{1,2,0:T(8,128)(2,1)}) %reduce-scatter.8.cloned.1.call-update) | async-done | bytes 691216 | tf_op jit(solution)/shard_map/reduce_scatter | solution.py:319
  (320 shorter events, 237.0 us)
Async XLA Ops:
  7.2 37.2 %all-gather.8.cloned.1.call-start = ((), (), s32[]{:S(2)}) async-start(), calls=%async_computation.8 | async-start | bytes 2985984 | tf_op jit(solution)/shard_map/all_gather | solution.py:89
  8.0 74.8 %all-gather.6.cloned.1.call-start = ((), (), s32[]{:S(2)}) async-start(), calls=%async_computation.7 | async-start | bytes 4644864 | tf_op jit(solution)/shard_map/all_gather | solution.py:96
  8.7 180.9 %all-gather.10.cloned.1.call-start = ((), (), s32[]{:S(2)}) async-start(), calls=%async_computation.10 | async-start | bytes 1990656 | tf_op jit(solution)/shard_map/all_gather | solution.py:92
  9.4 192.3 %all-reduce.8.cloned.1.call-start = ((), (), s32[]{:S(2)}) async-start(), calls=%async_computation.9 | async-start | bytes 3538944 | tf_op jit(solution)/shard_map/psum | solution.py:40
  113.3 107.6 %all-gather.12.cloned.1.call-start = ((), (), s32[]{:S(2)}) async-start(), calls=%async_computation.12 | async-start | bytes 2985984 | tf_op jit(solution)/shard_map/all_gather | solution.py:95
  113.3 10.6 %collective-permute-start = (bf16[144,1152]{1,0:T(8,128)(2,1)}, bf16[144,1152]{1,0:T(8,128)(2,1)}, u32[]{:S(2)}, u32[]{:S(2)}) collective-permute-start(bf16[144,1152]{1,0:T(8,128)(2,1)} %param.27), channel_id=1, source_target_pairs={{0,4},{4,8},{8,12},{12,16},{16,20},{20,24},{24,28},{28,0},{1,5},{5... | collective-permute-start | bytes 995336 | tf_op jit(solution)/shard_map/ppermute | solution.py:20
  113.4 37.9 %collective-permute-start.4 = (bf16[144,1152]{1,0:T(8,128)(2,1)}, bf16[144,1152]{1,0:T(8,128)(2,1)}, u32[]{:S(2)}, u32[]{:S(2)}) collective-permute-start(bf16[144,1152]{1,0:T(8,128)(2,1)} %param.27), channel_id=1, source_target_pairs={{0,28},{4,0},{8,4},{12,8},{16,12},{20,16},{24,20},{28,24},{1,29},{... | collective-permute-start | bytes 995336 | tf_op jit(solution)/shard_map/ppermute | solution.py:22
  116.0 183.3 %all-reduce.10.cloned.1.call-start = ((), (), s32[]{:S(2)}) async-start(), calls=%async_computation.11 | async-start | bytes 3538944 | tf_op jit(solution)/shard_map/psum | solution.py:40
  123.9 26.8 %collective-permute-start.1 = (bf16[144,1152]{1,0:T(8,128)(2,1)}, bf16[144,1152]{1,0:T(8,128)(2,1)}, u32[]{:S(2)}, u32[]{:S(2)}) collective-permute-start(bf16[144,1152]{1,0:T(8,128)(2,1)} %collective-permute-done), channel_id=1, source_target_pairs={{0,4},{4,8},{8,12},{12,16},{16,20},{20,24},{24,28},{28,0},{1,5},{5... | collective-permute-start | bytes 995336 | tf_op jit(solution)/shard_map/ppermute | solution.py:20
  150.8 10.1 collective-permute-start.2
  151.3 10.6 %collective-permute-start.5 = (bf16[144,1152]{1,0:T(8,128)(2,1)}, bf16[144,1152]{1,0:T(8,128)(2,1)S(1)}, u32[]{:S(2)}, u32[]{:S(2)}) collective-permute-start(bf16[144,1152]{1,0:T(8,128)(2,1)} %collective-permute-done.4), channel_id=1, source_target_pairs={{0,28},{4,0},{8,4},{12,8},{16,12},{20,16},{24,20},{28,24},{1,29},{... | collective-permute-start | bytes 995336 | tf_op jit(solution)/shard_map/ppermute | solution.py:22
  160.8 10.2 collective-permute-start.3
  161.9 18.4 %collective-permute-start.6 = (bf16[144,1152]{1,0:T(8,128)(2,1)S(1)}, bf16[144,1152]{1,0:T(8,128)(2,1)S(1)}, u32[]{:S(2)}, u32[]{:S(2)}) collective-permute-start(bf16[144,1152]{1,0:T(8,128)(2,1)S(1)} %collective-permute-done.5), channel_id=1, source_target_pairs={{0,28},{4,0},{8,4},{12,8},{16,12},{20,16},{24,20},{28,24},{1,29},{... | collective-permute-start | bytes 995336 | tf_op jit(solution)/shard_map/ppermute | solution.py:22
  218.0 175.8 %all-reduce.12.cloned.1.call-start = ((), (), s32[]{:S(2)}) async-start(), calls=%async_computation.13 | async-start | bytes 3538944 | tf_op jit(solution)/shard_map/psum | solution.py:40
  319.1 175.4 %all-reduce.14.cloned.1.call-start = ((), (), s32[]{:S(2)}) async-start(), calls=%async_computation.14 | async-start | bytes 3538944 | tf_op jit(solution)/shard_map/psum | solution.py:40
  419.8 135.6 %all-reduce.16.cloned.1.call-start = ((), (), s32[]{:S(2)}) async-start(), calls=%async_computation.15 | async-start | bytes 2949120 | tf_op jit(solution)/shard_map/psum | solution.py:295
  427.9 165.4 %reduce-scatter.16.cloned.1.call-start = ((), (), s32[]{:S(2)}) async-start(), calls=%async_computation.20 | async-start | bytes 995328 | tf_op jit(solution)/shard_map/reduce_scatter | solution.py:332
  430.9 200.8 %reduce-scatter.14.cloned.1.call-start = ((), (), s32[]{:S(2)}) async-start(), calls=%async_computation.19 | async-start | bytes 995328 | tf_op jit(solution)/shard_map/reduce_scatter | solution.py:329
  434.6 236.1 %reduce-scatter.12.cloned.1.call-start = ((), (), s32[]{:S(2)}) async-start(), calls=%async_computation.18 | async-start | bytes 995328 | tf_op jit(solution)/shard_map/reduce_scatter | solution.py:326
  505.7 212.4 %reduce-scatter.18.cloned.1.call-start = ((), (), s32[]{:S(2)}) async-start(), calls=%async_computation.21 | async-start | bytes 2985984 | tf_op jit(solution)/shard_map/reduce_scatter | solution.py:335
  510.6 254.9 %reduce-scatter.20.cloned.1.call-start = ((), (), s32[]{:S(2)}) async-start(), calls=%async_computation.22 | async-start | bytes 2985984 | tf_op jit(solution)/shard_map/reduce_scatter | solution.py:338
  515.5 387.1 %all-reduce.18.cloned.1.call-start = ((), (), s32[]{:S(2)}) async-start(), calls=%async_computation.23 | async-start | bytes 7077888 | tf_op jit(solution)/shard_map/psum | solution.py:40
  540.5 417.4 %reduce-scatter.10.cloned.1.call-start = ((), (), s32[]{:S(2)}) async-start(), calls=%async_computation.17 | async-start | bytes 2985984 | tf_op jit(solution)/shard_map/reduce_scatter | solution.py:323
  550.5 467.0 %reduce-scatter.8.cloned.1.call-start = ((), (), s32[]{:S(2)}) async-start(), calls=%async_computation.16 | async-start | bytes 4423680 | tf_op jit(solution)/shard_map/reduce_scatter | solution.py:319
  (62 other events, 1321.2 us)
Sparse Core Ops, SparseCore 0:
  10.0 34.4 all-gather.7
  46.3 36.4 all-gather.5
  84.7 26.5 all-gather.9
  114.1 75.5 all-reduce.7
  191.5 29.2 all-gather.11
  223.8 75.5 all-reduce.9
  319.3 74.5 all-reduce.11
  419.9 74.5 all-reduce.13
  497.8 57.6 all-reduce.15
  558.9 34.3 reduce-scatter.15
  596.5 35.0 reduce-scatter.13
  635.7 35.0 reduce-scatter.11
  674.2 43.7 reduce-scatter.17
  721.8 43.7 reduce-scatter.19
  768.4 134.1 all-reduce.17
  905.9 42.9 reduce-scatter.9
  951.2 66.3 reduce-scatter.7
